TPU v7x, 32 devices: a whole 2x2x4 slice. The times are simulated.
32 devices in a mesh: groups: 2 (over y), tm: 16 (over z, x, core).
Axes of the slice: x: 2, y: 2, z: 4, core: 2. Of those that a mesh axis runs over, the one named last changes fastest.
Arguments:
- positions: float32 [128, 3, 1536], P(('groups', 'tm')), parts along dimension 0, may hold values from -6 to 6
- atom_pairs: int32 [2, 8192], replicated, may hold values from 0 to 1535, as said below
- frame_counts: int32 [32], P('groups'), parts along dimension 0, may hold values from 1 to 4, as said below
Outputs:
- mean_now: float32 [16384], P('groups'), parts along dimension 0
- mean_lag: float32 [16384], P('groups'), parts along dimension 0
- cov_now: float32 [16384, 8192], P(('groups', 'tm')), parts along dimension 0
- cov_lag: float32 [16384, 8192], P(('groups', 'tm')), parts along dimension 0
There are 2 independent parts, one for each index of `groups`. A program takes and returns all parts, laid end to end along the dimension named above; an argument that names none is the same for every part. Nothing has to cross between parts.
Inputs may be any that keep to these rules, and one draw needn't show every extreme that they name: `atom_pairs`: the two atoms of a pair differ; every atom is the first atom of some pair. Each block's valid frames are its first frame_counts frames; in every draw one block holds 4 valid frames and another 1.
All inputs are finite; a program needn't handle non-finite values.
Results may differ from a plain program's by a relative error of at most 0.0029.
Values sent between devices are 32-bit elements; how exact they have to be, the bound alone decides.
A program may use at most 192 MiB of HBM per device.

v0:
```python
import math

import jax
import jax.numpy as jnp
from jax import lax
from jax.sharding import PartitionSpec as P

FR = 4
LAG = 1


def from_behind(block, axis, distance):
    devices = range(lax.axis_size(axis))
    route = [(i - distance, i) for i in devices if i - distance in devices]
    return lax.ppermute(block, axis, route)


def featurize(frames, atom_pairs):
    atoms_first = jnp.transpose(frames, (2, 1, 0))
    first_atom = jnp.take(atoms_first, atom_pairs[0], axis=0)
    second_atom = jnp.take(atoms_first, atom_pairs[1], axis=0)
    difference = first_atom - second_atom
    return jnp.sqrt(jnp.sum(difference * difference, axis=1))


def block_weights(frame_counts, block_number):
    blocks = frame_counts.shape[0]
    offsets = jnp.arange(FR, dtype=jnp.int32)
    current = frame_counts[block_number]
    following = jnp.where(
        block_number + 1 < blocks, frame_counts[jnp.minimum(block_number + 1, blocks - 1)], 0
    )
    ahead_index = offsets + LAG
    valid_now = offsets < current
    valid_ahead = jnp.where(ahead_index < FR, ahead_index < current, ahead_index - FR < following)
    return (valid_now & valid_ahead).astype(jnp.float32)


def many_weights(frame_counts, block_ids):

    def one_block(block_number):
        return block_weights(frame_counts, block_number)

    return jax.vmap(one_block)(block_ids).reshape(-1)


def centered(features, means):
    return (features - means[:, None]).astype(jnp.bfloat16)


def add_products(totals, early_cols, late_cols, weights, row_start, row_count):
    left_rows = lax.dynamic_slice_in_dim(early_cols, row_start, row_count, 0) * weights[
        None, :
    ].astype(jnp.bfloat16)
    contraction = (((1,), (1,)), ((), ()))
    now_part = lax.dot_general(
        left_rows, early_cols, contraction, preferred_element_type=jnp.float32
    )
    lag_part = lax.dot_general(
        left_rows, late_cols, contraction, preferred_element_type=jnp.float32
    )
    return (totals[0] + now_part, totals[1] + lag_part)


def lag_rim(positions):
    return from_behind(positions[:LAG], "tm", -1)


def shared_means(extended, atom_pairs, frame_counts, own_block):
    features = featurize(extended, atom_pairs)
    weights = block_weights(frame_counts, own_block)
    sum_now = jnp.sum(weights[None, :] * features[:, :FR], axis=1)
    sum_lag = jnp.sum(weights[None, :] * features[:, LAG:], axis=1)
    totals = lax.psum((sum_now, sum_lag, jnp.sum(weights)), "tm")
    return (totals[0] / totals[2], totals[1] / totals[2], totals[2])


def body(positions, atom_pairs, frame_counts):
    blocks = lax.axis_size("tm")
    own_block = lax.axis_index("tm")
    width = atom_pairs.shape[1]
    row_count = width // blocks
    row_start = own_block * row_count
    frame_span = FR + LAG
    zero_block = jnp.zeros((row_count, width), jnp.float32)
    extended = jnp.concatenate([positions, lag_rim(positions)], axis=0)
    mean_now, mean_lag, pair_count = shared_means(extended, atom_pairs, frame_counts, own_block)
    totals = (zero_block, zero_block)
    received = lax.all_gather(extended, "tm", axis=0, tiled=True)
    count_blocks = received.shape[0] // frame_span
    group_size = math.gcd(count_blocks, 8)
    arranged = received.reshape(
        count_blocks // group_size, group_size * frame_span, 3, received.shape[2]
    )

    def group_step(carried, group_index):
        frame_slab = lax.dynamic_index_in_dim(arranged, group_index, 0, keepdims=False)
        features = featurize(frame_slab, atom_pairs).reshape(width, group_size, frame_span)
        early_cols = centered(features[:, :, :FR].reshape(width, group_size * FR), mean_now)
        late_cols = centered(features[:, :, LAG:].reshape(width, group_size * FR), mean_lag)
        block_ids = group_index * group_size + jnp.arange(group_size, dtype=jnp.int32)
        weights = many_weights(frame_counts, block_ids)
        return (add_products(carried, early_cols, late_cols, weights, row_start, row_count), None)

    totals, unused_item = lax.scan(
        group_step, totals, jnp.arange(count_blocks // group_size, dtype=jnp.int32)
    )
    cov_now = totals[0] / pair_count
    cov_lag = totals[1] / pair_count
    return (mean_now, mean_lag, cov_now, cov_lag)


def solution(mesh):
    return jax.shard_map(
        body,
        mesh=mesh,
        in_specs=(P(("groups", "tm"), None, None), P(), P("groups")),
        out_specs=(P("groups"), P("groups"), P(("groups", "tm"), None), P(("groups", "tm"), None)),
        check_vma=False,
    )
```

profile of v0, /device:TPU:0, one launch (start us, length us, event | category | flops | bytes accessed | tf_op | source)
XLA Modules:
  0.0 729.8 jit_solution(7578302152603896713)
XLA Ops:
  7.2 0.0 all-gather.2.cloned.1.call-start
  7.2 0.9 slice.51
  8.1 1.3 collective-permute-start
  9.4 1.0 fusion.21
  10.5 1.3 fusion.22
  12.4 1.2 fusion.18
  13.7 3.4 copy.46
  17.1 2.7 copy.47
  19.9 3.7 fusion.24
  23.6 4.9 pad_maximum_fusion
  28.5 59.9 %gather_fusion.4 = f32[8192,3,5]{2,1,0:T(4,128)} fusion(f32[1536,3,5]{2,1,0:T(4,128)S(1)} %fusion.24, s32[8192]{0:T(1024)S(1)} %fusion.16), kind=kCustom, calls=%fused_computation.clone | custom fusion | bytes 1015808 | tf_op jit(solution)/shard_map/jit(_take)/gather | solution.py:20
  88.3 59.8 %gather_fusion.5 = f32[8192,3,5]{2,1,0:T(4,128)} fusion(f32[1536,3,5]{2,1,0:T(4,128)S(1)} %fusion.24, s32[8192]{0:T(1024)S(1)} %fusion.17), kind=kCustom, calls=%fused_computation.2.clone | custom fusion | bytes 1015808 | tf_op jit(solution)/shard_map/jit(_take)/gather | solution.py:21
  148.2 3.7 copy.49
  152.0 52.4 %fusion.13 = f32[8192,5]{1,0:T(8,128)} fusion(f32[8192,3,5]{2,1,0:T(4,128)} %gather_fusion.5, f32[8192,3,5]{2,1,0:T(4,128)} %gather_fusion.4, pred[8192]{0:T(1024)(128)(4,1)S(1)} %get-tuple-element.355, pred[8192]{0:T(1024)(128)(4,1)S(1)} %get-tuple-element.356), kind=kLoop, calls=%fused_computation.42 | loop fusion | flops 573440 | bytes 1163264 | tf_op jit(solution)/shard_map/reduce_sum | solution.py:23
  204.3 2.8 copy.48
  207.2 0.1 sqrt.16
  207.3 0.2 fusion.14
  207.5 66.2 %all-reduce.2 = (f32[8192]{0:T(1024)S(1)}, f32[]{:T(128)}, f32[8192]{0:T(1024)S(1)}) all-reduce(f32[8192]{0:T(1024)S(1)} %get-tuple-element.315, f32[]{:T(128)} %get-tuple-element.339, f32[8192]{0:T(1024)S(1)} %get-tuple-element.314), channel_id=1, replica_groups=mesh['groups'=2,'tm'=16] {'tm'}, use_global_device_ids=true, to_apply=%region_2.4 | all-reduce | flops 16385 | bytes 131080 | tf_op jit(solution)/shard_map/psum | solution.py:74
  273.7 0.6 broadcast_divide_fusion.2
  274.3 0.6 broadcast_divide_fusion.3
  274.8 0.0 all-gather.2.cloned.1.call-done
  274.9 423.7 %while.17 = (s32[]{:T(128)}, f32[512,8192]{1,0:T(8,128)}, f32[512,8192]{1,0:T(8,128)}, s32[2]{0:T(128)S(1)}, f32[2,40,3,1536]{3,2,1,0:T(4,128)}, /*index=5*/s32[...) while((s32[]{:T(128)}, f32[512,8192]{1,0:T(8,128)}, ...), condition=%wide.region_9.12_spmd.clone, body=%wide.region_7.11_spmd.clone.sunk | while | flops 559581568 | bytes 114927528 | solution.py:105
  274.9 0.6 dynamic_slice.53
  277.4 2.3 constant_dynamic-slice_fusion.2
  279.8 2.8 copy.57
  282.6 0.1 fusion.33
  282.6 59.8 %gather_fusion = f32[8192,3,40]{2,1,0:T(4,128)} fusion(f32[1536,3,40]{2,1,0:T(4,128)S(1)} %bitcast.36, s32[8192]{0:T(1024)S(1)} %fusion.34), kind=kCustom, calls=%fused_computation.3.clone.clone.1 | custom fusion | bytes 7897088 | tf_op jit(solution)/shard_map/while/body/eval_jaxpr/jit(_take)/gather | solution.py:21
  342.5 59.9 %gather_fusion.1 = f32[8192,3,40]{2,1,0:T(4,128)} fusion(f32[1536,3,40]{2,1,0:T(4,128)S(1)} %bitcast.37, s32[8192]{0:T(1024)S(1)} %fusion.35), kind=kCustom, calls=%fused_computation.1.clone.clone.1 | custom fusion | bytes 7897088 | tf_op jit(solution)/shard_map/while/body/eval_jaxpr/jit(_take)/gather | solution.py:20
  402.4 52.4 %fusion.36 = f32[8192,40]{1,0:T(8,128)} fusion(f32[8192,3,40]{2,1,0:T(4,128)} %gather_fusion, f32[8192,3,40]{2,1,0:T(4,128)} %gather_fusion.1, pred[8192]{0:T(1024)(128)(4,1)S(1)} %get-tuple-element.430, pred[8192]{0:T(1024)(128)(4,1)S(1)} %get-tuple-element.431), kind=kLoop, calls=%fused_computation.8.clone.1 | loop fusion | flops 4587520 | bytes 9191424 | tf_op jit(solution)/shard_map/while/body/eval_jaxpr/reduce_sum | solution.py:23
  454.7 2.8 copy.58
  457.6 0.3 sqrt.21
  457.9 0.2 sqrt.22
  458.1 1.5 fusion.37
  459.5 1.6 reshape.298
  461.1 0.1 subtract_convert_fusion.6
  461.2 0.4 reshape.300
  462.3 0.6 gather_fusion.3
  462.9 0.6 gather_fusion.2
  463.6 0.1 convert_convert_fusion.2
  463.7 0.1 reshape.299
  463.8 8.6 %select_add_fusion.5 = f32[512,8192]{1,0:T(8,128)} fusion(f32[512,8192]{1,0:T(8,128)} %get-tuple-element.454, pred[]{:T(512)S(6)} %compare.3, f32[8192,32]{0,1:T(8,128)S(1)} %reshape.300, f32[8192]{0:T(1024)S(1)} %get-tuple-element.475, bf16[8192,32]{0,1:T(8,128)(2,1)S(1)} %subtract_convert_fusion.6, s32[]{:T(128)} %get-tuple-element.473, ...), kind=kOutput, calls=%fused_computation.9.clone.1 | convolution fusion | flops 277413888 | bytes 34669060 | tf_op jit(solution)/shard_map/while/body/eval_jaxpr/dot_general | solution.py:59
  472.4 8.6 %select_add_fusion.4 = f32[512,8192]{1,0:T(8,128)} fusion(f32[512,8192]{1,0:T(8,128)} %get-tuple-element.453, bf16[8192,32]{0,1:T(8,128)(2,1)S(1)} %subtract_convert_fusion.6, pred[]{:T(512)S(6)} %compare.3, s32[]{:T(128)} %get-tuple-element.473, bf16[32]{0:T(256)(128)(2,1)S(1)} %reshape.299), kind=kOutput, calls=%fused_computation.10.clone.1 | convolution fusion | flops 276889600 | bytes 34112004 | tf_op jit(solution)/shard_map/while/body/eval_jaxpr/dot_general | solution.py:56
  481.0 0.6 dynamic_slice.53
  483.5 2.3 constant_dynamic-slice_fusion.2
  485.8 2.8 copy.57
  488.6 0.1 fusion.33
  488.7 59.8 %gather_fusion = f32[8192,3,40]{2,1,0:T(4,128)} fusion(f32[1536,3,40]{2,1,0:T(4,128)S(1)} %bitcast.36, s32[8192]{0:T(1024)S(1)} %fusion.34), kind=kCustom, calls=%fused_computation.3.clone.clone.1 | custom fusion | bytes 7897088 | tf_op jit(solution)/shard_map/while/body/eval_jaxpr/jit(_take)/gather | solution.py:21
  548.5 59.9 %gather_fusion.1 = f32[8192,3,40]{2,1,0:T(4,128)} fusion(f32[1536,3,40]{2,1,0:T(4,128)S(1)} %bitcast.37, s32[8192]{0:T(1024)S(1)} %fusion.35), kind=kCustom, calls=%fused_computation.1.clone.clone.1 | custom fusion | bytes 7897088 | tf_op jit(solution)/shard_map/while/body/eval_jaxpr/jit(_take)/gather | solution.py:20
  608.4 52.4 %fusion.36 = f32[8192,40]{1,0:T(8,128)} fusion(f32[8192,3,40]{2,1,0:T(4,128)} %gather_fusion, f32[8192,3,40]{2,1,0:T(4,128)} %gather_fusion.1, pred[8192]{0:T(1024)(128)(4,1)S(1)} %get-tuple-element.430, pred[8192]{0:T(1024)(128)(4,1)S(1)} %get-tuple-element.431), kind=kLoop, calls=%fused_computation.8.clone.1 | loop fusion | flops 4587520 | bytes 9191424 | tf_op jit(solution)/shard_map/while/body/eval_jaxpr/reduce_sum | solution.py:23
  660.8 2.8 copy.58
  663.6 0.3 sqrt.21
  663.9 0.2 sqrt.22
  664.1 1.5 fusion.37
  665.6 1.6 reshape.298
  667.2 0.1 subtract_convert_fusion.6
  667.3 0.4 reshape.300
  668.3 0.6 gather_fusion.3
  669.0 0.6 gather_fusion.2
  669.6 0.1 convert_convert_fusion.2
  669.7 0.1 reshape.299
  669.8 14.4 %select_add_fusion.5 = f32[512,8192]{1,0:T(8,128)} fusion(f32[512,8192]{1,0:T(8,128)} %get-tuple-element.454, pred[]{:T(512)S(6)} %compare.3, f32[8192,32]{0,1:T(8,128)S(1)} %reshape.300, f32[8192]{0:T(1024)S(1)} %get-tuple-element.475, bf16[8192,32]{0,1:T(8,128)(2,1)S(1)} %subtract_convert_fusion.6, s32[]{:T(128)} %get-tuple-element.473, ...), kind=kOutput, calls=%fused_computation.9.clone.1 | convolution fusion | flops 277413888 | bytes 34669060 | tf_op jit(solution)/shard_map/while/body/eval_jaxpr/dot_general | solution.py:59
  684.2 14.4 %select_add_fusion.4 = f32[512,8192]{1,0:T(8,128)} fusion(f32[512,8192]{1,0:T(8,128)} %get-tuple-element.453, bf16[8192,32]{0,1:T(8,128)(2,1)S(1)} %subtract_convert_fusion.6, pred[]{:T(512)S(6)} %compare.3, s32[]{:T(128)} %get-tuple-element.473, bf16[32]{0:T(256)(128)(2,1)S(1)} %reshape.299), kind=kOutput, calls=%fused_computation.10.clone.1 | convolution fusion | flops 276889600 | bytes 34112004 | tf_op jit(solution)/shard_map/while/body/eval_jaxpr/dot_general | solution.py:56
  698.6 12.2 %broadcast_divide_fusion = f32[512,8192]{1,0:T(8,128)} fusion(f32[512,8192]{1,0:T(8,128)} %get-tuple-element.210, f32[]{:T(128)} %get-tuple-element.337), kind=kLoop, calls=%fused_computation.43 | loop fusion | flops 4194304 | bytes 33554436 | tf_op jit(solution)/shard_map/div | solution.py:109
  710.8 12.2 %broadcast_divide_fusion.1 = f32[512,8192]{1,0:T(8,128)} fusion(f32[512,8192]{1,0:T(8,128)} %get-tuple-element.209, f32[]{:T(128)} %get-tuple-element.337), kind=kLoop, calls=%fused_computation.44 | loop fusion | flops 4194304 | bytes 33554436 | tf_op jit(solution)/shard_map/div | solution.py:108
  (34 shorter events, 0.3 us)
Async XLA Ops:
  7.2 267.7 %all-gather.2.cloned.1.call-start = ((), (), s32[]{:S(2)}) async-start(), calls=%async_computation | async-start | bytes 2088960 | tf_op jit(solution)/shard_map/all_gather | solution.py:89
  8.1 9.0 %collective-permute-start = (f32[1,3,1536]{2,0,1:T(1,128)S(1)}, f32[1,3,1536]{2,0,1:T(1,128)S(1)}, u32[]{:S(2)}, u32[]{:S(2)}) collective-permute-start(f32[1,3,1536]{2,0,1:T(1,128)S(1)} %slice.51), channel_id=1, source_target_pairs={{1,0},{2,1},{3,2},{4,3},{5,4},{6,5},{7,6},{8,7},{9,8},{10,9},{11,1... | collective-permute-start | bytes 55304 | tf_op jit(solution)/shard_map/ppermute | solution.py:15
  151.9 123.0 %copy-start = (s32[16]{0:T(128)S(1)}, s32[16]{0:T(128)}, u32[]{:S(2)}) copy-start(s32[16]{0:T(128)} %param.11) | copy-start | bytes 196
  151.9 123.0 %copy-start.1 = (s32[2,8192]{1,0:T(2,128)S(1)}, s32[2,8192]{1,0:T(2,128)}, u32[]{:S(2)}) copy-start(s32[2,8192]{1,0:T(2,128)} %param.10) | copy-start | bytes 196612
  698.6 12.2 %copy-start.2 = (f32[8192]{0:T(1024)}, f32[8192]{0:T(1024)S(1)}, u32[]{:S(2)}) copy-start(f32[8192]{0:T(1024)S(1)} %get-tuple-element.482) | copy-start | bytes 98308
  698.6 12.2 %copy-start.3 = (f32[8192]{0:T(1024)}, f32[8192]{0:T(1024)S(1)}, u32[]{:S(2)}) copy-start(f32[8192]{0:T(1024)S(1)} %get-tuple-element.483) | copy-start | bytes 98308
Sparse Core Ops, SparseCore 0:
  152.1 44.5 all-gather.1
where the time goes:
time: 731 us; the launch traced here: 730 us
  local copies, waits for them, and re-layouts  403 us (55%)
  other arithmetic  193 us (26%)
  blocking collectives  66.2 us (9%)
  matrix products  46 us (6%)
  between operations  14.8 us (2%)
    gather x3, local copies, waits for them, and re-layouts, featurize(): first_atom = jnp.take(atoms_first, atom_pairs[0], axis=0)  180 us
    gather x3, local copies, waits for them, and re-layouts, featurize(): second_atom = jnp.take(atoms_first, atom_pairs[1], axis=0)  179 us
    reduce_sum x3, other arithmetic, featurize(): return jnp.sqrt(jnp.sum(difference * difference, axis=1))  157 us
    psum x1, blocking collectives, shared_means(): totals = lax.psum((sum_now, sum_lag, jnp.sum(weights)), 'tm')  66.2 us
    dot_general x2, matrix products, add_products(): lax.dot_general(left_rows, late_cols, contraction, preferred_element_type...  23 us
    dot_general x2, matrix products, add_products(): lax.dot_general(left_rows, early_cols, contraction, preferred_element_typ...  23 us
  transfers between devices with their start and end apart: 2, of which 0 were waited for; matrix products, arithmetic and copies ran while one was open for 9% of the time, Pallas kernels for 0%

commit v1 on v0

v1 whole, which is shorter than its diff:
```python
import functools

import jax
import jax.numpy as jnp
from jax import lax
from jax.experimental import pallas as pl
from jax.experimental.pallas import tpu as pltpu
from jax.sharding import PartitionSpec as P

FR = 4
LAG = 1


def axis_split(devices):
    cores = 2 if devices % 2 == 0 else 1
    chips = devices // cores
    x = 1
    while x * x * x * 8 <= chips and chips % (x * 2) == 0:
        x *= 2
    return chips // x, x, cores


def gather_kernel(sizes, own_ref, all_ref, local_sem, send_sem, recv_sem):
    zs, xs, cs = sizes
    me = lax.axis_index("tm")
    core = lax.rem(me, cs)
    x = lax.rem(me // cs, xs)
    z = me // (cs * xs)

    def index(zi, xi, ci):
        return (zi * xs + xi) * cs + ci

    z_peers = [lax.rem(z + d, zs) for d in range(1, zs)]
    x_peers = [lax.rem(x + d, xs) for d in range(1, xs)]
    c_peers = [lax.rem(core + d, cs) for d in range(1, cs)]
    targets = (
        [index(p, x, core) for p in z_peers]
        + [index(z, p, core) for p in x_peers]
        + [index(z, x, p) for p in c_peers]
    )
    barrier = pltpu.get_barrier_semaphore()
    for target in targets:
        pl.semaphore_signal(
            barrier, inc=1, device_id={"tm": target}, device_id_type=pl.DeviceIdType.MESH
        )
    pl.semaphore_wait(barrier, len(targets))

    sent = []

    def send(source, block, target):
        copy = pltpu.make_async_remote_copy(
            src_ref=source,
            dst_ref=all_ref.at[block],
            send_sem=send_sem.at[len(sent)],
            recv_sem=recv_sem.at[block],
            device_id={"tm": target},
            device_id_type=pl.DeviceIdType.MESH,
        )
        copy.start()
        sent.append(copy)

    def arrived(block):
        pltpu.make_async_remote_copy(
            src_ref=all_ref.at[block],
            dst_ref=all_ref.at[block],
            send_sem=send_sem.at[0],
            recv_sem=recv_sem.at[block],
            device_id={"tm": me},
            device_id_type=pl.DeviceIdType.MESH,
        ).wait_recv()

    for p in z_peers:
        send(own_ref, me, index(p, x, core))
    for p in x_peers:
        send(own_ref, me, index(z, p, core))
    for p in c_peers:
        send(own_ref, me, index(z, x, p))
    local = pltpu.make_async_copy(own_ref, all_ref.at[me], local_sem)
    local.start()
    for zi in z_peers:
        block = index(zi, x, core)
        arrived(block)
        for p in x_peers:
            send(all_ref.at[block], block, index(z, p, core))
        for p in c_peers:
            send(all_ref.at[block], block, index(z, x, p))
    for zi in [z] + z_peers:
        for xi in x_peers:
            block = index(zi, xi, core)
            arrived(block)
            for p in c_peers:
                send(all_ref.at[block], block, index(z, x, p))
    for zi in [z] + z_peers:
        for xi in [x] + x_peers:
            for ci in c_peers:
                arrived(index(zi, xi, ci))
    local.wait()
    for copy in sent:
        copy.wait_send()


def gather_blocks(block, devices):
    sizes = axis_split(devices)
    zs, xs, cs = sizes
    sends = (zs - 1) + zs * (xs - 1) + zs * xs * (cs - 1)
    return pl.pallas_call(
        functools.partial(gather_kernel, sizes),
        out_shape=jax.ShapeDtypeStruct((devices,) + block.shape, block.dtype),
        in_specs=[pl.BlockSpec(memory_space=pl.ANY)],
        out_specs=pl.BlockSpec(memory_space=pl.ANY),
        scratch_shapes=[
            pltpu.SemaphoreType.DMA,
            pltpu.SemaphoreType.DMA((max(sends, 1),)),
            pltpu.SemaphoreType.DMA((devices,)),
        ],
        compiler_params=pltpu.CompilerParams(collective_id=0, has_side_effects=True),
        name="gather_positions",
    )(block)


def shifted_up(rows):
    return jnp.concatenate([rows[LAG:], jnp.zeros((LAG, rows.shape[1]), rows.dtype)], axis=0)


def covariance_kernel(
    frames,
    row_count,
    counts_ref,
    positions_ref,
    pairs_ref,
    mean_now_ref,
    mean_lag_ref,
    cov_now_ref,
    cov_lag_ref,
    split_ref,
    weights_ref,
    left_ref,
):
    step = pl.program_id(0)
    chunk = cov_now_ref.shape[1]
    atoms = positions_ref.shape[3]

    def features_of(start, width):
        atom = lax.broadcasted_iota(jnp.int32, (atoms, width), 0)
        first = pairs_ref[0:1, pl.ds(start, width)]
        second = pairs_ref[1:2, pl.ds(start, width)]
        select = jnp.where(atom == first, 1.0, jnp.where(atom == second, -1.0, 0.0)).astype(
            jnp.bfloat16
        )
        parts = jnp.dot(split_ref[...], select, preferred_element_type=jnp.float32)
        rows = 3 * frames
        difference = parts[:rows] + (parts[rows : 2 * rows] + parts[2 * rows :])
        squares = difference * difference
        return jnp.sqrt(
            squares[:frames] + squares[frames : 2 * frames] + squares[2 * frames :]
        )

    def scale():
        return 1.0 / jnp.sum(weights_ref[...], axis=0, keepdims=True)

    def widened(row, width):
        return jnp.concatenate([row] * (width // 128), axis=1)

    def means_of(features, ahead):
        width = features.shape[1]
        weights = widened(weights_ref[...], width)
        pair_count = jnp.sum(weights, axis=0, keepdims=True)
        mean_now = jnp.sum(weights * features, axis=0, keepdims=True) / pair_count
        mean_lag = jnp.sum(weights * ahead, axis=0, keepdims=True) / pair_count
        return mean_now, mean_lag

    @pl.when(step == 0)
    def _():
        for c in range(3):
            values = positions_ref[:, c, :, :].reshape(frames, atoms)
            high = values.astype(jnp.bfloat16)
            rest = values - high.astype(jnp.float32)
            middle = rest.astype(jnp.bfloat16)
            low = (rest - middle.astype(jnp.float32)).astype(jnp.bfloat16)
            for s, part in enumerate((high, middle, low)):
                split_ref[pl.ds((3 * s + c) * frames, frames), :] = part
        frame = lax.broadcasted_iota(jnp.int32, (frames, 128), 0)

        def add_block(b, current):
            return jnp.where(frame // FR == b, counts_ref[b], current)

        current = lax.fori_loop(0, frames // FR, add_block, jnp.zeros((frames, 128), jnp.int32))
        valid = jnp.where(frame % FR < current, 1.0, 0.0)
        weights_ref[...] = valid * shifted_up(valid)

        own_width = max(row_count, 128)
        own_start = lax.axis_index("tm") * row_count
        base = pl.multiple_of(own_start // own_width * own_width, own_width)
        features = features_of(base, own_width)
        mean_now, _unused = means_of(features, shifted_up(features))
        early = (features - mean_now).astype(jnp.bfloat16).astype(jnp.float32)
        left = early * widened(weights_ref[...], own_width)
        left_ref[...] = jnp.transpose(left).astype(jnp.bfloat16)

    features = features_of(pl.multiple_of(step * chunk, chunk), chunk)
    ahead = shifted_up(features)
    mean_now, mean_lag = means_of(features, ahead)
    mean_now_ref[...] = mean_now
    mean_lag_ref[...] = mean_lag
    early = (features - mean_now).astype(jnp.bfloat16)
    late = (ahead - mean_lag).astype(jnp.bfloat16)
    if row_count == left_ref.shape[0]:
        left = left_ref[...]
    else:
        offset = lax.rem(lax.axis_index("tm") * row_count, left_ref.shape[0])
        left = left_ref[pl.ds(pl.multiple_of(offset, row_count), row_count), :]
    factor = widened(scale(), chunk)
    cov_now_ref[...] = jnp.dot(left, early, preferred_element_type=jnp.float32) * factor
    cov_lag_ref[...] = jnp.dot(left, late, preferred_element_type=jnp.float32) * factor


def covariances(positions, atom_pairs, frame_counts, row_count):
    devices, _, block_frames, atoms = positions.shape
    frames = devices * block_frames
    width = atom_pairs.shape[1]
    chunk = 512 if frames <= 128 else 128
    row = jax.ShapeDtypeStruct((1, width), jnp.float32)
    matrix = jax.ShapeDtypeStruct((row_count, width), jnp.float32)
    return pl.pallas_call(
        functools.partial(covariance_kernel, frames, row_count),
        out_shape=(row, row, matrix, matrix),
        grid=(width // chunk,),
        in_specs=[
            pl.BlockSpec(memory_space=pltpu.SMEM),
            pl.BlockSpec(positions.shape, lambda i: (0, 0, 0, 0), pipeline_mode=pl.Buffered(1)),
            pl.BlockSpec((2, width), lambda i: (0, 0), pipeline_mode=pl.Buffered(1)),
        ],
        out_specs=(
            pl.BlockSpec((1, chunk), lambda i: (0, i)),
            pl.BlockSpec((1, chunk), lambda i: (0, i)),
            pl.BlockSpec((row_count, chunk), lambda i: (0, i)),
            pl.BlockSpec((row_count, chunk), lambda i: (0, i)),
        ),
        scratch_shapes=[
            pltpu.VMEM((9 * frames, atoms), jnp.bfloat16),
            pltpu.VMEM((frames, 128), jnp.float32),
            pltpu.VMEM((max(row_count, 128), frames), jnp.bfloat16),
        ],
        compiler_params=pltpu.CompilerParams(vmem_limit_bytes=60 * 1024 * 1024),
        name="covariances",
    )(frame_counts, positions, atom_pairs)


def body(positions, atom_pairs, frame_counts):
    devices = lax.axis_size("tm")
    width = atom_pairs.shape[1]
    gathered = gather_blocks(jnp.transpose(positions, (1, 0, 2)), devices)
    mean_now, mean_lag, cov_now, cov_lag = covariances(
        gathered, atom_pairs, frame_counts, width // devices
    )
    return (mean_now.reshape(width), mean_lag.reshape(width), cov_now, cov_lag)


def solution(mesh):
    return jax.shard_map(
        body,
        mesh=mesh,
        in_specs=(P(("groups", "tm"), None, None), P(), P("groups")),
        out_specs=(P("groups"), P("groups"), P(("groups", "tm"), None), P(("groups", "tm"), None)),
        check_vma=False,
    )
```

time: 731 us -> 50.9 us (0.07)
  local copies, waits for them, and re-layouts: 403 us -> 0 us
  other arithmetic: 193 us -> 0 us
  blocking collectives: 66.2 us -> 0 us
  Pallas kernels: 0 us -> 50.1 us
  matrix products: 46 us -> 0 us
  between operations: 14.8 us -> 0.64 us
    gather x10 -> x0, local copies, waits for them, and re-layouts: 362 us -> none  [the longest x3 180 us: featurize(): first_atom = jnp.take(atoms_first, atom_pairs[0], axis=0)]
    reduce_sum x5 -> x0, other arithmetic: 159 us -> none  [the longest x3 157 us: featurize(): return jnp.sqrt(jnp.sum(difference * difference, axis=1))]
    psum x1 -> x0, blocking collectives: 66.2 us -> none  [shared_means(): totals = lax.psum((sum_now, sum_lag, jnp.sum(weights)), 'tm')]
    pallas_call x0 -> x2, Pallas kernels: none -> 50.1 us  [the longest x1 30.5 us: covariances(): pl.pallas_call(functools.partial(covariance_kernel, frames, row_count), o...]
    dot_general x4 -> x0, matrix products: 46 us -> none  [the longest x2 23 us: add_products(): lax.dot_general(left_rows, late_cols, contraction, preferred_element_type...]
    div x4 -> x0, other arithmetic: 25.6 us -> none  [the longest x1 12.2 us: body(): cov_now = totals[0] / pair_count]
    dynamic_slice x7 -> x0, local copies, waits for them, and re-layouts: 12.7 us -> none  [the longest x4 10.2 us: group_step(): lax.dynamic_index_in_dim(arranged, group_index, 0, keepdims=False)]
    reduce_sum x3 -> x0, local copies, waits for them, and re-layouts: 8.43 us -> none  [featurize(): return jnp.sqrt(jnp.sum(difference * difference, axis=1))]
  transfers between devices with their start and end apart: 2 -> 0, of which waited for: 0 -> 0; matrix products, arithmetic and copies ran while one was open for 9% -> 0% of each run, Pallas kernels for 0% -> 0%
where the time goes in v1:
time: 50.9 us; the launch traced here: 50.7 us
  Pallas kernels  50.1 us (98%)
  between operations  0.64 us (1%)
    pallas_call x1, Pallas kernels, covariances(): pl.pallas_call(functools.partial(covariance_kernel, frames, row_count), o...  30.5 us
    pallas_call x1, Pallas kernels, gather_blocks(): pl.pallas_call(functools.partial(gather_kernel, sizes), out_shape=jax.Sha...  19.6 us

profile of v1, /device:TPU:0, one launch (start us, length us, event | category | flops | bytes accessed | tf_op | source)
XLA Modules:
  0.0 50.7 jit_solution(15022373139504880555)
XLA Ops:
  0.6 19.6 %gather_positions.1.positions_ref = f32[16,3,4,1536]{3,2,1,0:T(4,128)} custom-call(f32[3,4,1536]{2,1,0:T(4,128)} %bitcast.3), custom_call_target="tpu_custom_call" | custom-call | tf_op jit(solution)/shard_map/gather_positions/pallas_call | solution.py:106
  20.2 30.5 %covariances.1 = (f32[1,8192]{1,0:T(1,128)}, f32[1,8192]{1,0:T(1,128)}, f32[512,8192]{1,0:T(8,128)}, f32[512,8192]{1,0:T(8,128)}) custom-call(s32[16]{0:T(128)} %counts_ref.1, f32[16,3,4,1536]{3,2,1,0:T(4,128)} %gather_positions.1.positions_ref, s32[2,8192]{1,0:T(2,128)} %pairs_ref.1), custom_call_target="tpu_custom_call" | custom-call | tf_op jit(solution)/shard_map/covariances/pallas_call | solution.py:224

commit v2 on v1

v2 whole, which is shorter than its diff:
```python
import functools

import jax
import jax.numpy as jnp
from jax import lax
from jax.experimental import pallas as pl
from jax.experimental.pallas import tpu as pltpu
from jax.sharding import PartitionSpec as P

FR = 4
LAG = 1
CORES = 2


def axis_split(devices):
    chips = devices // CORES
    x = 1
    while x * x * x * 8 <= chips and chips % (x * 2) == 0:
        x *= 2
    return chips // x, x


def features_kernel(
    sizes,
    own_ref,
    pairs_ref,
    features_ref,
    blocks_ref,
    select_ref,
    split_ref,
    result_ref,
    local_sem,
    send_sem,
    recv_sem,
    keep_sem,
    share_sem,
    fetch_sem,
):
    zs, xs = sizes
    me = lax.axis_index("tm")
    core = lax.rem(me, CORES)
    x = lax.rem(me // CORES, xs)
    z = me // (CORES * xs)
    chunks, atoms, width = select_ref.shape
    frames = blocks_ref.shape[0] * FR

    def device(zi, xi, ci):
        return {"tm": (zi * xs + xi) * CORES + ci}

    sibling = device(z, x, 1 - core)
    above = z + 1 < zs
    below = z > 0
    x_peers = [lax.rem(x + d, xs) for d in range(1, xs)]

    barrier = pltpu.get_barrier_semaphore()

    def greet(target):
        pl.semaphore_signal(
            barrier, inc=1, device_id=target, device_id_type=pl.DeviceIdType.MESH
        )

    @pl.when(above)
    def _():
        greet(device(z + 1, x, core))

    @pl.when(below)
    def _():
        greet(device(z - 1, x, core))

    for p in x_peers:
        greet(device(z, p, core))
    greet(sibling)
    local = pltpu.make_async_copy(own_ref, blocks_ref.at[z * xs + x], local_sem)
    local.start()
    met = above.astype(jnp.int32) + below.astype(jnp.int32) + len(x_peers) + 1
    pl.semaphore_wait(barrier, met)

    sent = []

    def send(source, block, target, allowed):
        copy = pltpu.make_async_remote_copy(
            src_ref=source,
            dst_ref=blocks_ref.at[block],
            send_sem=send_sem.at[len(sent)],
            recv_sem=recv_sem.at[block],
            device_id=target,
            device_id_type=pl.DeviceIdType.MESH,
        )
        sent.append((copy, allowed))
        if allowed is None:
            copy.start()
        else:
            pl.when(allowed)(copy.start)

    def arrived(block):
        pltpu.make_async_remote_copy(
            src_ref=blocks_ref.at[block],
            dst_ref=blocks_ref.at[block],
            send_sem=send_sem.at[0],
            recv_sem=recv_sem.at[block],
            device_id=sibling,
            device_id_type=pl.DeviceIdType.MESH,
        ).wait_recv()

    def build_select(j, carry):
        atom = lax.broadcasted_iota(jnp.int32, (atoms, width), 0)
        start = pl.multiple_of(j * width, width)
        first = pairs_ref[0:1, pl.ds(start, width)]
        second = pairs_ref[1:2, pl.ds(start, width)]
        select_ref[j] = jnp.where(
            atom == first, 1.0, jnp.where(atom == second, -1.0, 0.0)
        ).astype(jnp.bfloat16)
        return carry

    built = [chunks * d // zs for d in range(zs + 1)]

    def build_some(d):
        lax.fori_loop(built[d], built[d + 1], build_select, 0)

    mine = z * xs + x
    send(own_ref, mine, device(z + 1, x, core), above)
    send(own_ref, mine, device(z - 1, x, core), below)
    for p in x_peers:
        send(own_ref, mine, device(z, p, core), None)
    for d in range(1, zs):
        build_some(d - 1)
        for sign in (-1, 1):
            origin = z + sign * d
            exists = origin >= 0 if sign < 0 else origin < zs
            block = origin * xs + x
            pl.when(exists)(functools.partial(arrived, block))
            if d < zs - 1:
                onward = above if sign < 0 else below
                send(
                    blocks_ref.at[block],
                    block,
                    device(z - sign, x, core),
                    jnp.logical_and(exists, onward),
                )
            for p in x_peers:
                send(blocks_ref.at[block], block, device(z, p, core), exists)
    build_some(zs - 1)
    for zi in range(zs):
        for p in x_peers:
            arrived(zi * xs + p)
    local.wait()

    for c in range(3):
        values = blocks_ref[:, c, :, :].reshape(frames, atoms)
        high = values.astype(jnp.bfloat16)
        rest = values - high.astype(jnp.float32)
        middle = rest.astype(jnp.bfloat16)
        low = (rest - middle.astype(jnp.float32)).astype(jnp.bfloat16)
        for s, part in enumerate((high, middle, low)):
            split_ref[pl.ds((3 * s + c) * frames, frames), :] = part

    def keep(j):
        return pltpu.make_async_copy(
            result_ref.at[j], features_ref.at[core, j], keep_sem.at[j]
        )

    def share(j):
        return pltpu.make_async_remote_copy(
            src_ref=result_ref.at[j],
            dst_ref=features_ref.at[core, j],
            send_sem=share_sem.at[j],
            recv_sem=fetch_sem.at[j],
            device_id=sibling,
            device_id_type=pl.DeviceIdType.MESH,
        )

    def publish(j):
        keep(j).start()
        share(j).start()

    def featurize(j):
        parts = jnp.dot(split_ref[...], select_ref[j], preferred_element_type=jnp.float32)
        rows = 3 * frames
        difference = parts[:rows] + (parts[rows : 2 * rows] + parts[2 * rows :])
        squares = difference * difference
        result_ref[j] = jnp.sqrt(
            squares[:frames] + squares[frames : 2 * frames] + squares[2 * frames :]
        )

    def step(j, carry):
        featurize(j)
        publish(j - 1)
        return carry

    featurize(0)
    lax.fori_loop(1, chunks, step, 0)
    publish(chunks - 1)

    def finish(j, carry):
        keep(j).wait()
        share(j).wait_send()
        share(j).wait_recv()
        return carry

    lax.fori_loop(0, chunks, finish, 0)
    for copy, allowed in sent:
        if allowed is None:
            copy.wait_send()
        else:
            pl.when(allowed)(copy.wait_send)


def shared_features(block, atom_pairs, devices, chunk):
    zs, xs = axis_split(devices)
    held = devices // CORES
    frames = held * FR
    atoms = block.shape[2]
    chunks = atom_pairs.shape[1] // chunk
    sends = 2 + (xs - 1) + 2 * (zs - 1) * xs
    dma = pltpu.SemaphoreType.DMA
    return pl.pallas_call(
        functools.partial(features_kernel, (zs, xs)),
        out_shape=jax.ShapeDtypeStruct((CORES, chunks, frames, chunk), jnp.float32),
        in_specs=[
            pl.BlockSpec(memory_space=pl.ANY),
            pl.BlockSpec(memory_space=pltpu.VMEM),
        ],
        out_specs=pl.BlockSpec(memory_space=pl.ANY),
        scratch_shapes=[
            pltpu.VMEM((held,) + block.shape, jnp.float32),
            pltpu.VMEM((chunks, atoms, chunk), jnp.bfloat16),
            pltpu.VMEM((9 * frames, atoms), jnp.bfloat16),
            pltpu.VMEM((chunks, frames, chunk), jnp.float32),
            dma,
            dma((sends,)),
            dma((held,)),
            dma((chunks,)),
            dma((chunks,)),
            dma((chunks,)),
        ],
        compiler_params=pltpu.CompilerParams(
            collective_id=0, has_side_effects=True, vmem_limit_bytes=60 * 1024 * 1024
        ),
        name="features",
    )(block, atom_pairs)


def moved(rows, by):
    zeros = jnp.zeros((abs(by), rows.shape[1]), rows.dtype)
    if by > 0:
        return jnp.concatenate([rows[by:], zeros], axis=0)
    return jnp.concatenate([zeros, rows[:by]], axis=0)


def next_frames(even, odd):
    last = lax.broadcasted_iota(jnp.int32, even.shape, 0) % FR == FR - LAG
    up = moved(even, 1)
    ahead_even = jnp.where(last, moved(odd, 1 - FR), up)
    ahead_odd = jnp.where(last, up, moved(odd, 1))
    return jnp.concatenate([ahead_even, ahead_odd], axis=0)


def covariance_kernel(
    row_count,
    counts_ref,
    features_ref,
    mean_now_ref,
    mean_lag_ref,
    cov_now_ref,
    cov_lag_ref,
    weights_ref,
    left_ref,
):
    step = pl.program_id(0)
    _, _, frames, width = features_ref.shape

    def widened(rows):
        return jnp.concatenate([rows] * (width // 128), axis=1)

    def frames_of(j):
        even = features_ref[0, j]
        odd = features_ref[1, j]
        return jnp.concatenate([even, odd], axis=0), next_frames(even, odd)

    def pair_count():
        return jnp.sum(weights_ref[...], axis=0, keepdims=True)

    def mean_of(rows):
        total = jnp.sum(widened(weights_ref[...]) * rows, axis=0, keepdims=True)
        return total / widened(pair_count())

    @pl.when(step == 0)
    def _():
        frame = lax.broadcasted_iota(jnp.int32, (frames, 128), 0)

        def valid_of(core):
            def add_block(b, current):
                return jnp.where(frame // FR == b, counts_ref[CORES * b + core], current)

            current = lax.fori_loop(
                0, frames // FR, add_block, jnp.zeros((frames, 128), jnp.int32)
            )
            return jnp.where(frame % FR < current, 1.0, 0.0)

        even = valid_of(0)
        odd = valid_of(1)
        weights_ref[...] = jnp.concatenate([even, odd], axis=0) * next_frames(even, odd)
        start = lax.axis_index("tm") * row_count
        features, _unused = frames_of(start // width)
        early = (features - mean_of(features)).astype(jnp.bfloat16).astype(jnp.float32)
        left = early * widened(weights_ref[...])
        left_ref[...] = jnp.transpose(left).astype(jnp.bfloat16)

    features, ahead = frames_of(step)
    mean_now = mean_of(features)
    mean_lag = mean_of(ahead)
    mean_now_ref[...] = mean_now
    mean_lag_ref[...] = mean_lag
    early = (features - mean_now).astype(jnp.bfloat16)
    late = (ahead - mean_lag).astype(jnp.bfloat16)
    if row_count == width:
        left = left_ref[...]
    else:
        offset = lax.rem(lax.axis_index("tm") * row_count, width)
        left = left_ref[pl.ds(pl.multiple_of(offset, row_count), row_count), :]
    factor = widened(1.0 / pair_count())
    cov_now_ref[...] = jnp.dot(left, early, preferred_element_type=jnp.float32) * factor
    cov_lag_ref[...] = jnp.dot(left, late, preferred_element_type=jnp.float32) * factor


def covariances(features, frame_counts, row_count):
    _, chunks, frames, chunk = features.shape
    width = chunks * chunk
    row = jax.ShapeDtypeStruct((1, width), jnp.float32)
    matrix = jax.ShapeDtypeStruct((row_count, width), jnp.float32)
    return pl.pallas_call(
        functools.partial(covariance_kernel, row_count),
        out_shape=(row, row, matrix, matrix),
        grid=(chunks,),
        in_specs=[
            pl.BlockSpec(memory_space=pltpu.SMEM),
            pl.BlockSpec(
                features.shape, lambda i: (0, 0, 0, 0), pipeline_mode=pl.Buffered(1)
            ),
        ],
        out_specs=(
            pl.BlockSpec((1, chunk), lambda i: (0, i)),
            pl.BlockSpec((1, chunk), lambda i: (0, i)),
            pl.BlockSpec((row_count, chunk), lambda i: (0, i)),
            pl.BlockSpec((row_count, chunk), lambda i: (0, i)),
        ),
        scratch_shapes=[
            pltpu.VMEM((CORES * frames, 128), jnp.float32),
            pltpu.VMEM((chunk, CORES * frames), jnp.bfloat16),
        ],
        compiler_params=pltpu.CompilerParams(vmem_limit_bytes=60 * 1024 * 1024),
        name="covariances",
    )(frame_counts, features)


def body(positions, atom_pairs, frame_counts):
    devices = lax.axis_size("tm")
    width = atom_pairs.shape[1]
    row_count = width // devices
    chunk = 512 if devices <= 32 else 128
    features = shared_features(
        jnp.transpose(positions, (1, 0, 2)), atom_pairs, devices, chunk
    )
    mean_now, mean_lag, cov_now, cov_lag = covariances(features, frame_counts, row_count)
    return (mean_now.reshape(width), mean_lag.reshape(width), cov_now, cov_lag)


def solution(mesh):
    return jax.shard_map(
        body,
        mesh=mesh,
        in_specs=(P(("groups", "tm"), None, None), P(), P("groups")),
        out_specs=(P("groups"), P("groups"), P(("groups", "tm"), None), P(("groups", "tm"), None)),
        check_vma=False,
    )
```

time: 50.9 us -> 47.5 us (0.933)
  Pallas kernels: 50.1 us -> 46.7 us
    pallas_call x2, Pallas kernels: 50.1 us -> 46.7 us  [the longest x1 30.7 us: shared_features(): pl.pallas_call(functools.partial(features_kernel, (zs, xs)), out_shape=ja...]
where the time goes in v2:
time: 47.5 us; the launch traced here: 47.3 us
  Pallas kernels  46.7 us (98%)
  between operations  0.64 us (1%)
    pallas_call x1, Pallas kernels, shared_features(): pl.pallas_call(functools.partial(features_kernel, (zs, xs)), out_shape=ja...  30.7 us
    pallas_call x1, Pallas kernels, covariances(): pl.pallas_call(functools.partial(covariance_kernel, row_count), out_shape...  16 us

profile of v2, /device:TPU:0, one launch (start us, length us, event | category | flops | bytes accessed | tf_op | source)
XLA Modules:
  0.0 47.3 jit_solution(16492935998551255375)
XLA Ops:
  0.6 30.7 %features.1.features_ref = f32[2,16,32,512]{3,2,1,0:T(8,128)} custom-call(f32[3,4,1536]{2,1,0:T(4,128)} %bitcast.3, s32[2,8192]{1,0:T(2,128)} %pairs_ref.1), custom_call_target="tpu_custom_call" | custom-call | tf_op jit(solution)/shard_map/features/pallas_call | solution.py:216
  31.4 16.0 %covariances.1 = (f32[1,8192]{1,0:T(1,128)}, f32[1,8192]{1,0:T(1,128)}, f32[512,8192]{1,0:T(8,128)}, f32[512,8192]{1,0:T(8,128)}) custom-call(s32[16]{0:T(128)} %counts_ref.1, f32[2,16,32,512]{3,2,1,0:T(8,128)} %features.1.features_ref), custom_call_target="tpu_custom_call" | custom-call | tf_op jit(solution)/shard_map/covariances/pallas_call | solution.py:331

commit v3 on v2

--- a/solution.py
+++ b/solution.py
@@ -103,13 +103,12 @@
         ).wait_recv()
 
     def build_select(j, carry):
-        atom = lax.broadcasted_iota(jnp.int32, (atoms, width), 0)
+        atom = lax.broadcasted_iota(jnp.int32, (atoms, width), 0).astype(jnp.int16)
         start = pl.multiple_of(j * width, width)
-        first = pairs_ref[0:1, pl.ds(start, width)]
-        second = pairs_ref[1:2, pl.ds(start, width)]
-        select_ref[j] = jnp.where(
-            atom == first, 1.0, jnp.where(atom == second, -1.0, 0.0)
-        ).astype(jnp.bfloat16)
+        first = pairs_ref[0:1, pl.ds(start, width)].astype(jnp.int16)
+        second = pairs_ref[1:2, pl.ds(start, width)].astype(jnp.int16)
+        one, zero = jnp.bfloat16(1.0), jnp.bfloat16(0.0)
+        select_ref[j] = jnp.where(atom == first, one, jnp.where(atom == second, -one, zero))
         return carry
 
     built = [chunks * d // zs for d in range(zs + 1)]

time: 47.5 us -> 47.5 us (level)
  no operation moved by 1% of the time
where the time goes in v3:
time: 47.5 us; the launch traced here: 47.3 us
  Pallas kernels  46.7 us (98%)
  between operations  0.64 us (1%)
    pallas_call x1, Pallas kernels, shared_features(): pl.pallas_call(functools.partial(features_kernel, (zs, xs)), out_shape=ja...  30.7 us
    pallas_call x1, Pallas kernels, covariances(): pl.pallas_call(functools.partial(covariance_kernel, row_count), out_shape...  16 us

profile of v3, /device:TPU:0, one launch (start us, length us, event | category | flops | bytes accessed | tf_op | source)
XLA Modules:
  0.0 47.3 jit_solution(9169023759075972391)
XLA Ops:
  0.6 30.7 %features.1.features_ref = f32[2,16,32,512]{3,2,1,0:T(8,128)} custom-call(f32[3,4,1536]{2,1,0:T(4,128)} %bitcast.3, s32[2,8192]{1,0:T(2,128)} %pairs_ref.1), custom_call_target="tpu_custom_call" | custom-call | tf_op jit(solution)/shard_map/features/pallas_call | solution.py:215
  31.4 16.0 %covariances.1 = (f32[1,8192]{1,0:T(1,128)}, f32[1,8192]{1,0:T(1,128)}, f32[512,8192]{1,0:T(8,128)}, f32[512,8192]{1,0:T(8,128)}) custom-call(s32[16]{0:T(128)} %counts_ref.1, f32[2,16,32,512]{3,2,1,0:T(8,128)} %features.1.features_ref), custom_call_target="tpu_custom_call" | custom-call | tf_op jit(solution)/shard_map/covariances/pallas_call | solution.py:330
